TPU v7x, 512 devices: a whole 4x8x8 slice. The times are simulated.
512 devices in a mesh: seq: 8 (over z), exp: 64 (over x, y, core).
Axes of the slice: x: 4, y: 8, z: 8, core: 2. Of those that a mesh axis runs over, the one named last changes fastest.
Arguments:
- tokens: bfloat16 [65536, 4096], P(('seq', 'exp')), may hold values from -6 to 6
- cotangent: bfloat16 [65536, 4096], P(('seq', 'exp')), may hold values from -3 to 3
- factors: bfloat16 [64, 3, 4, 1024, 128], P('exp', None, None, 'seq'), may hold values from -0.09375 to 0.09375
- mix: float32 [64, 3, 4, 4, 4], P('exp'), may hold values from -3 to 3
- selection: int32 [64, 16, 64], P('exp', 'seq'), may hold values from 0 to 4095, as said below
- scores: int32 [64, 16, 64], P('exp', 'seq'), may hold values from -192 to 191
Outputs:
- token_grad: bfloat16 [65536, 4096], P(('seq', 'exp'))
- factor_grad: float32 [64, 3, 4, 1024, 128], P('exp', None, None, 'seq')
- mix_grad: float32 [64, 3, 4, 4, 4], P('exp')
- gate_grad: float32 [64, 16, 64], P('exp', 'seq')
Inputs may be any that keep to these rules, and one draw needn't show every extreme that they name: `selection`: for every expert and block the 64 positions are distinct and ascending; at most 3 of them lie among the 128 positions of one device (aligned runs of 128), and for every expert and block some device holds exactly 3 of them.
All inputs are finite; a program needn't handle non-finite values.
Results may differ from a plain program's by a relative error of at most 0.015.
Values may be sent and summed in bfloat16 or wider, within the bound.
A program may use at most 64 MiB of HBM per device.

v0:
```python
import jax
import jax.numpy as jnp
from jax import lax
from jax.sharding import PartitionSpec as P

C = 64
PICKS = 1


PRECISE = lax.Precision.HIGHEST


def expand(mixing, factor_set):
    count_f, rows_f, cols_f = factor_set.shape
    total = jnp.zeros((count_f, rows_f, count_f, cols_f), jnp.float32)
    for number in range(count_f):
        total = (
            total
            + mixing[number][:, None, :, None]
            * factor_set[number].astype(jnp.float32)[None, :, None, :]
        )
    return total.reshape(count_f * rows_f, count_f * cols_f).astype(jnp.bfloat16)


def factored_grads(mixing, factor_set, left, right):
    count_f, rows_f, cols_f = factor_set.shape
    slots = left.shape[0]
    left_view = left.reshape(slots, count_f, rows_f)
    right_view = right.reshape(slots, count_f, cols_f)
    mixed_right = jnp.einsum(
        "iab,rbq->riaq", mixing, right_view.astype(jnp.float32), precision=PRECISE
    )
    factor_out = jnp.einsum(
        "rap,riaq->ipq", left_view.astype(jnp.float32), mixed_right, precision=PRECISE
    )
    through = jnp.einsum("rap,ipq->riaq", left_view, factor_set, preferred_element_type=jnp.float32)
    mixing_out = jnp.einsum(
        "riaq,rbq->iab", through, right_view.astype(jnp.float32), precision=PRECISE
    )
    return (factor_out, mixing_out)


def silu_parts(preact):
    sigmoid_val = jax.nn.sigmoid(preact)
    return (preact * sigmoid_val, sigmoid_val + preact * sigmoid_val * (1.0 - sigmoid_val))


def contract(left, right):
    return lax.dot_general(
        left, right, (((0,), (0,)), ((), ())), preferred_element_type=jnp.float32
    )


def transposed(left, kernel):
    return lax.dot_general(
        left, kernel, (((1,), (1,)), ((), ())), preferred_element_type=jnp.float32
    )


def shards(tokens, cotangent, factors, mix, selection, scores):
    peer_count = lax.axis_size("exp")
    own_rows = tokens.shape[0]
    model_width = tokens.shape[1]
    slot_cap = 3 * PICKS * own_rows // (2 * peer_count)
    block_len = peer_count * C // PICKS
    slot_total = peer_count * slot_cap
    chosen = selection[0]
    position = (jnp.arange(chosen.shape[0], dtype=jnp.int32)[:, None] * block_len + chosen).reshape(
        -1
    )
    owner_idx = position // own_rows
    local_row = position % own_rows
    row_count = position.shape[0]
    earlier = jnp.sum((owner_idx[None, :] < owner_idx[:, None]).astype(jnp.int32), axis=1)
    slot_of = owner_idx * slot_cap + jnp.arange(row_count, dtype=jnp.int32) - earlier
    slot_hits = slot_of[:, None] == jnp.arange(slot_total, dtype=jnp.int32)[None, :]
    wanted = jnp.sum(jnp.where(slot_hits, local_row[:, None] + 1, 0), axis=0) - 1
    requested = lax.all_to_all(
        wanted.reshape(peer_count, slot_cap), "exp", split_axis=0, concat_axis=0, tiled=True
    )
    pick_rows = (
        requested.reshape(-1)[:, None] == jnp.arange(own_rows, dtype=jnp.int32)[None, :]
    ).astype(jnp.bfloat16)
    send_rows = (
        jnp.dot(pick_rows, tokens, preferred_element_type=jnp.float32)
        .astype(jnp.bfloat16)
        .reshape(peer_count, slot_cap, model_width)
    )
    send_grads = (
        jnp.dot(pick_rows, cotangent, preferred_element_type=jnp.float32)
        .astype(jnp.bfloat16)
        .reshape(peer_count, slot_cap, model_width)
    )
    gathered = lax.all_gather(factors, "seq", axis=3, tiled=True)[0]
    kernels = [expand(mix[0, number], gathered[number]) for number in range(3)]
    gate_val = jax.nn.sigmoid(scores[0].reshape(-1).astype(jnp.float32) / 64.0)
    got_rows, got_grads = (
        lax.all_to_all(send_rows, "exp", split_axis=0, concat_axis=0, tiled=True),
        lax.all_to_all(send_grads, "exp", split_axis=0, concat_axis=0, tiled=True),
    )
    sel_rows = jnp.take(got_rows.reshape(slot_total, model_width), slot_of, axis=0)
    pre_gate = jnp.dot(sel_rows, kernels[0], preferred_element_type=jnp.float32)
    pre_up = jnp.dot(sel_rows, kernels[1], preferred_element_type=jnp.float32)
    gate_act, gate_slope = silu_parts(pre_gate)
    hidden = (gate_act * pre_up).astype(jnp.bfloat16)
    expert_out = transposed(hidden, kernels[2])
    sel_grads = jnp.take(got_grads.reshape(slot_total, model_width), slot_of, axis=0)
    gate_in = jnp.sum(sel_grads.astype(jnp.float32) * expert_out, axis=1)
    gate_grad = gate_in * gate_val * (1.0 - gate_val)
    out_grad = (gate_val[:, None] * sel_grads.astype(jnp.float32)).astype(jnp.bfloat16)
    hidden_grad = jnp.dot(out_grad, kernels[2], preferred_element_type=jnp.float32)
    gate_pre = (hidden_grad * pre_up * gate_slope).astype(jnp.bfloat16)
    up_pre = (hidden_grad * gate_act).astype(jnp.bfloat16)
    row_grad = (transposed(gate_pre, kernels[0]) + transposed(up_pre, kernels[1])).astype(
        jnp.bfloat16
    )
    back_rows = (
        contract(slot_hits.astype(jnp.bfloat16), row_grad)
        .astype(jnp.bfloat16)
        .reshape(peer_count, slot_cap, model_width)
    )
    returned = lax.all_to_all(back_rows, "exp", split_axis=0, concat_axis=0, tiled=True)
    token_grad = contract(pick_rows, returned.reshape(slot_total, model_width)).astype(jnp.bfloat16)
    operand_pairs = [(sel_rows, gate_pre), (sel_rows, up_pre), (out_grad, hidden)]
    projected = [
        factored_grads(
            mix[0, number], gathered[number], operand_pairs[number][0], operand_pairs[number][1]
        )
        for number in range(3)
    ]
    factor_part = jnp.stack([item[0] for item in projected])[None]
    mix_part = jnp.stack([item[1] for item in projected])[None]
    factor_grad = lax.psum_scatter(
        factor_part.astype(jnp.bfloat16), "seq", scatter_dimension=3, tiled=True
    ).astype(jnp.float32)
    mix_grad = lax.psum(mix_part, "seq")
    return (token_grad, factor_grad, mix_grad, gate_grad.reshape(1, -1, C))


def solution(mesh):
    return jax.shard_map(
        shards,
        mesh=mesh,
        in_specs=(
            P(("seq", "exp"), None),
            P(("seq", "exp"), None),
            P("exp", None, None, "seq", None),
            P("exp", None, None, None, None),
            P("exp", "seq", None),
            P("exp", "seq", None),
        ),
        out_specs=(
            P(("seq", "exp"), None),
            P("exp", None, None, "seq", None),
            P("exp", None, None, None, None),
            P("exp", "seq", None),
        ),
        check_vma=False,
    )
```

profile of v0, /device:TPU:1, one launch (start us, length us, event | category | flops | bytes accessed | tf_op | source)
XLA Modules:
  0.0 298.6 jit_solution(9856022250247314939)
XLA Ops:
  7.3 0.1 add.154
  7.3 0.8 squeeze.14
  8.2 0.2 convert_reduce_fusion
  8.4 0.1 select_reduce_fusion
  8.5 0.1 sub.29
  8.7 20.7 %all_to_all.21 = s32[64,1,3]{2,1,0:T(1,128)S(1)} all-to-all(s32[64,1,3]{2,1,0:T(1,128)S(1)} %bitcast.255), channel_id=1, replica_groups=mesh['seq'=8,'exp'=64] {'exp'}, dimensions={0} | all-to-all | bytes 1536 | tf_op jit(solution)/shard_map/all_to_all | solution.py:78
  29.4 0.5 broadcast.231
  29.9 0.7 reduce.3
  30.6 0.1 eq.33
  30.8 0.6 convolution_convert_fusion.1
  31.4 2.3 reshape.423
  33.8 4.8 %all-to-all-start.2 = ((bf16[64,3,4096]{2,1,0:T(4,128)(2,1)}), bf16[64,3,4096]{2,1,0:T(4,128)(2,1)S(1)}, u32[]{:S(2)}, u32[]{:S(2)}) async-start(bf16[64,3,4096]{2,1,0:T(4,128)(2,1)} %reshape.423), calls=%async_computation.2 | async-start | bytes 4194304 | tf_op jit(solution)/shard_map/all_to_all | solution.py:98
  38.6 0.7 all-gather.2.cloned.1.call-update
  39.3 1.9 convolution_convert_fusion.2
  41.2 4.1 %reshape.421 = bf16[64,3,4096]{2,1,0:T(4,128)(2,1)} reshape(bf16[192,4096]{1,0:T(8,128)(2,1)} %convolution_convert_fusion.2) | data formatting | bytes 3145728 | tf_op jit(solution)/shard_map/reshape | solution.py:92
  45.3 44.7 %all-to-all-done.2 = bf16[64,3,4096]{2,1,0:T(4,128)(2,1)S(1)} async-done(((bf16[64,3,4096]{2,1,0:T(4,128)(2,1)}), bf16[64,3,4096]{2,1,0:T(4,128)(2,1)S(1)}, u32[]{:S(2)}, u32[]{:S(2)}) %all-to-all-start.2) | async-done | bytes 1572896 | tf_op jit(solution)/shard_map/all_to_all | solution.py:98
  89.9 6.0 %all-to-all-start.1 = ((bf16[64,3,4096]{2,1,0:T(4,128)(2,1)}), bf16[64,3,4096]{2,1,0:T(4,128)(2,1)}, u32[]{:S(2)}, u32[]{:S(2)}) async-start(bf16[64,3,4096]{2,1,0:T(4,128)(2,1)} %reshape.421), calls=%async_computation.1 | async-start | bytes 4194304 | tf_op jit(solution)/shard_map/all_to_all | solution.py:99
  95.9 0.2 reduce-scatter.4.cloned.1.call-start
  96.2 3.1 %reshape.424 = bf16[192,4096]{1,0:T(8,128)(2,1)S(1)} reshape(bf16[64,3,4096]{2,1,0:T(4,128)(2,1)} %copy-done.4) | data formatting | bytes 3145728 | tf_op jit(solution)/shard_map/reshape | solution.py:101
  99.4 2.2 gather_fusion.1
  101.5 45.6 %all-to-all-done.1 = bf16[64,3,4096]{2,1,0:T(4,128)(2,1)} async-done(((bf16[64,3,4096]{2,1,0:T(4,128)(2,1)}), bf16[64,3,4096]{2,1,0:T(4,128)(2,1)}, u32[]{:S(2)}, u32[]{:S(2)}) %all-to-all-start.1) | async-done | bytes 1572896 | tf_op jit(solution)/shard_map/all_to_all | solution.py:99
  147.1 3.1 %reshape.422 = bf16[192,4096]{1,0:T(8,128)(2,1)S(1)} reshape(bf16[64,3,4096]{2,1,0:T(4,128)(2,1)} %all-to-all-done.1) | data formatting | bytes 3145728 | tf_op jit(solution)/shard_map/reshape | solution.py:107
  150.2 2.2 gather_fusion
  152.4 1.4 broadcast_select_fusion
  153.9 3.3 %fusion.49 = (f32[1024,128]{1,0:T(8,128)S(1)}, f32[1024,128]{1,0:T(8,128)S(1)}, f32[1024,128]{1,0:T(8,128)S(1)}, f32[1024,128]{1,0:T(8,128)S(1)}, f32[1024,128]{...) fusion(bf16[1,3,4,1024,128]{4,3,2,1,0:T(8,128)(2,1)} %all-gathe, ...), kind=kLoop, calls=%fused_computation.89 | loop fusion | flops 1572864 | bytes 9437184 | tf_op jit(solution)/shard_map/convert_element_type | solution.py:20
  157.1 9.1 %add_convert_fusion = (bf16[4,1024,4,128]{3,2,1,0:T(4,128)(2,1)S(1)}, bf16[4,1024,4,128]{3,2,1,0:T(4,128)(2,1)S(1)}) fusion(f32[1024,128]{1,0:T(8,128)S(1)} %get-tuple-element.28, f32[4,4]{1,0:T(4,128)S(1)} %get-tuple-element.42, f32[1024,128]{1,0:T(8,128)S(1)} %get-tuple-element.29, f32[4,4]{1,0:T(4,128)S(1)} %get-tuple-element.43, ...), kind=kLoop, calls=%fused_computation.2 | loop fusion | flops 33554432 | bytes 12583424 | tf_op jit(solution)/shard_map/convert.21
  166.2 0.8 fusion.3
  167.0 1.2 copy-done.14
  168.2 1.5 multiply_convert_fusion
  169.7 5.9 %add_convert_fusion.2 = bf16[4,1024,4,128]{3,2,1,0:T(4,128)(2,1)S(1)} fusion(f32[1024,128]{1,0:T(8,128)S(1)} %get-tuple-element.36, f32[4,4]{1,0:T(4,128)S(1)} %get-tuple-element.50, f32[1024,128]{1,0:T(8,128)} %get-tuple-element.37, f32[4,4]{1,0:T(4,128)S(1)} %get-tuple-element.51, f32[1024,128]{1,0:T(8,128)} %get-tuple-element.38, ...), kind=kLoop, calls=%fused_computation.4 | loop fusion | flops 16777216 | bytes 6291712 | tf_op jit(solution)/shard_map/convert.23
  175.7 1.9 copy-done.5
  177.6 1.6 fusion.23
  179.3 0.6 subtract_multiply_fusion
  180.0 0.3 fusion.17
  180.3 0.9 convolution_bitcast_fusion.3
  181.3 3.7 %multiply_convert_fusion.1 = (bf16[128,512]{1,0:T(8,128)(2,1)S(1)}, bf16[128,512]{1,0:T(8,128)(2,1)}) fusion(f32[128,512]{1,0:T(8,128)} %copy-done.14, f32[128,512]{1,0:T(8,128)} %get-tuple-element.54, bf16[128,4096]{1,0:T(8,128)(2,1)S(1)} %fusion.17, bf16[512,8,4,128]{3,2,1,0:T(4,128)(2,1)} %bitcast.250), kind=kOutput, calls=%fused_computation.91 | convolution fusion | flops 537657344 | bytes 6029312 | tf_op jit(solution)/shard_map/dot_general | solution.py:111
  185.0 2.6 convolution_bitcast_fusion.4
  187.6 0.9 reshape.470
  188.6 1.6 convolution_bitcast_fusion.5
  190.2 3.2 %fusion.21 = bf16[1,1,4,1024,128]{3,4,2,1,0:T(8,128)(2,1)S(1)} fusion(f32[128,4,4,128]{3,2,1,0:T(4,128)} %convolution_bitcast_fusion.4, bf16[16,4,8,1024]{3,2,1,0:T(8,128)(2,1)S(1)} %bitcast.241), kind=kOutput, calls=%fused_computation.35 | convolution fusion | flops 3221749760 | bytes 3145728 | tf_op jit(solution)/shard_map/rap,riaq->ipq/dot_general | solution.py:33
  193.4 2.0 fusion.20
  195.4 2.0 fusion.22
  197.4 2.1 pad_maximum_fusion
  199.5 6.0 %copy.73 = bf16[1,3,4,1024,128]{4,2,1,0,3:T(4,128)(2,1)} copy(bf16[1,3,4,1024,128]{3,4,2,1,0:T(8,128)(2,1)} %pad_maximum_fusion) | data formatting | bytes 6291456
  205.5 6.4 %reshape.494 = bf16[1024,1536]{1,0:T(8,128)(2,1)} reshape(bf16[1024,1,3,4,128]{4,3,2,1,0:T(4,128)(2,1)} %bitcast.247) | data formatting | bytes 6291456
  211.9 5.0 %fusion.1 = f32[128,4096]{1,0:T(8,128)} fusion(bf16[128,512]{1,0:T(8,128)(2,1)S(1)} %copy-done.11, bf16[512,8,4,128]{3,2,1,0:T(4,128)(2,1)} %bitcast.246), kind=kOutput, calls=%fused_computation.12 | convolution fusion | flops 536870912 | bytes 6422528 | tf_op jit(solution)/shard_map/dot_general | solution.py:55
  216.9 6.0 %convolution_convert_fusion = bf16[192,4096]{1,0:T(8,128)(2,1)} fusion(f32[128,4096]{1,0:T(8,128)} %fusion.1, bf16[128,512]{1,0:T(8,128)(2,1)S(1)} %get-tuple-element.39, bf16[512,8,4,128]{3,2,1,0:T(4,128)(2,1)} %bitcast.244, s32[128]{0:T(128)S(1)} %get-tuple-element.24), kind=kOutput, calls=%fused_computation.5 | convolution fusion | flops 740057088 | bytes 7995904 | tf_op jit(solution)/shard_map/dot_general | solution.py:49
  222.9 4.1 %reshape.425 = bf16[64,3,4096]{2,1,0:T(4,128)(2,1)} reshape(bf16[192,4096]{1,0:T(8,128)(2,1)} %convolution_convert_fusion) | data formatting | bytes 3145728 | tf_op jit(solution)/shard_map/reshape | solution.py:120
  227.0 6.0 %all-to-all-start.3 = ((bf16[64,3,4096]{2,1,0:T(4,128)(2,1)}), bf16[64,3,4096]{2,1,0:T(4,128)(2,1)}, u32[]{:S(2)}, u32[]{:S(2)}) async-start(bf16[64,3,4096]{2,1,0:T(4,128)(2,1)} %reshape.425), calls=%async_computation.3 | async-start | bytes 4194304 | tf_op jit(solution)/shard_map/all_to_all | solution.py:122
  233.0 0.8 reshape.428
  233.8 0.8 reshape.431
  234.7 2.1 convolution_bitcast_fusion
  236.8 2.2 convolution_bitcast_fusion.6
  239.0 0.7 convolution_bitcast_fusion.1
  239.7 2.2 convolution_bitcast_fusion.7
  241.9 0.7 convolution_bitcast_fusion.2
  242.6 2.2 convolution_bitcast_fusion.8
  244.8 32.7 %psum.7 = f32[1,3,4,4,4]{4,3,2,1,0:T(4,128)} all-reduce(f32[1,3,4,4,4]{4,3,2,1,0:T(4,128)S(1)} %maximum_bitcast_fusion), channel_id=1, replica_groups=mesh['seq'=8,'exp'=64] {'seq'}, use_global_device_ids=true, to_apply=%region_3.5 | all-reduce | flops 192 | bytes 1536 | tf_op jit(solution)/shard_map/psum | solution.py:136
  277.5 6.7 %all-to-all-done.3 = bf16[64,3,4096]{2,1,0:T(4,128)(2,1)} async-done(((bf16[64,3,4096]{2,1,0:T(4,128)(2,1)}), bf16[64,3,4096]{2,1,0:T(4,128)(2,1)}, u32[]{:S(2)}, u32[]{:S(2)}) %all-to-all-start.3) | async-done | bytes 1572896 | tf_op jit(solution)/shard_map/all_to_all | solution.py:122
  284.2 3.1 %reshape.426 = bf16[192,4096]{1,0:T(8,128)(2,1)S(1)} reshape(bf16[64,3,4096]{2,1,0:T(4,128)(2,1)} %all-to-all-done.3) | data formatting | bytes 3145728 | tf_op jit(solution)/shard_map/reshape | solution.py:123
  287.3 1.5 convolution_convert_fusion.3
  288.9 1.1 reshape.495
  290.0 0.3 copy.74
  290.3 1.1 copy.54
  (46 shorter events, 0.5 us)
Async XLA Ops:
  7.2 23.6 %copy-start = (bf16[128,4096]{1,0:T(8,128)(2,1)S(1)}, bf16[128,4096]{1,0:T(8,128)(2,1)}, u32[]{:S(2)}) copy-start(bf16[128,4096]{1,0:T(8,128)(2,1)} %param.8) | copy-start | bytes 3145732
  31.4 7.9 %copy-start.8 = (bf16[128,4096]{1,0:T(8,128)(2,1)S(1)}, bf16[128,4096]{1,0:T(8,128)(2,1)}, u32[]{:S(2)}) copy-start(bf16[128,4096]{1,0:T(8,128)(2,1)} %param.9) | copy-start | bytes 3145732
  33.8 56.2 %all-to-all-start.2 = ((bf16[64,3,4096]{2,1,0:T(4,128)(2,1)}), bf16[64,3,4096]{2,1,0:T(4,128)(2,1)S(1)}, u32[]{:S(2)}, u32[]{:S(2)}) async-start(bf16[64,3,4096]{2,1,0:T(4,128)(2,1)} %reshape.423), calls=%async_computation.2 | async-start | bytes 4194304 | tf_op jit(solution)/shard_map/all_to_all | solution.py:98
  38.6 115.3 %all-gather.2.cloned.1.call-start = ((), (), s32[]{:S(2)}) async-start(), calls=%async_computation.5 | async-start | bytes 3538944 | tf_op jit(solution)/shard_map/all_gather | solution.py:94
  41.2 55.0 %copy-start.12 = (f32[1,3,4,4,4]{4,3,2,1,0:T(4,128)S(1)}, f32[1,3,4,4,4]{4,3,2,1,0:T(4,128)}, u32[]{:S(2)}) copy-start(f32[1,3,4,4,4]{4,3,2,1,0:T(4,128)} %param.11) | copy-start | bytes 2308
  89.9 6.3 %copy-start.4 = (bf16[64,3,4096]{2,1,0:T(4,128)(2,1)}, bf16[64,3,4096]{2,1,0:T(4,128)(2,1)S(1)}, u32[]{:S(2)}) copy-start(bf16[64,3,4096]{2,1,0:T(4,128)(2,1)S(1)} %all-to-all-done.2) | copy-start | bytes 4718596
  89.9 57.2 %all-to-all-start.1 = ((bf16[64,3,4096]{2,1,0:T(4,128)(2,1)}), bf16[64,3,4096]{2,1,0:T(4,128)(2,1)}, u32[]{:S(2)}, u32[]{:S(2)}) async-start(bf16[64,3,4096]{2,1,0:T(4,128)(2,1)} %reshape.421), calls=%async_computation.1 | async-start | bytes 4194304 | tf_op jit(solution)/shard_map/all_to_all | solution.py:99
  95.9 192.9 %reduce-scatter.4.cloned.1.call-start = ((), (), s32[]{:S(2)}) async-start(), calls=%async_computation.6 | async-start | bytes 3538944
  166.2 3.5 %copy-start.2 = (bf16[4,1024,4,128]{3,2,1,0:T(4,128)(2,1)}, bf16[4,1024,4,128]{3,2,1,0:T(4,128)(2,1)S(1)}, u32[]{:S(2)}) copy-start(bf16[4,1024,4,128]{3,2,1,0:T(4,128)(2,1)S(1)} %get-tuple-element.56) | copy-start | bytes 12582916
  166.2 3.5 %copy-start.3 = (bf16[4,1024,4,128]{3,2,1,0:T(4,128)(2,1)}, bf16[4,1024,4,128]{3,2,1,0:T(4,128)(2,1)S(1)}, u32[]{:S(2)}) copy-start(bf16[4,1024,4,128]{3,2,1,0:T(4,128)(2,1)S(1)} %get-tuple-element.55) | copy-start | bytes 12582916
  167.0 1.2 copy-start.14
  169.7 7.9 %copy-start.6 = (bf16[128,4096]{1,0:T(8,128)(2,1)S(1)}, bf16[128,4096]{1,0:T(8,128)(2,1)}, u32[]{:S(2)}) copy-start(bf16[128,4096]{1,0:T(8,128)(2,1)} %gather_fusion) | copy-start | bytes 3145732
  175.7 1.9 copy-start.5
  175.7 3.6 %copy-start.13 = (s32[1,2,64]{2,1,0:T(2,128)S(1)}, s32[1,2,64]{2,1,0:T(2,128)}, u32[]{:S(2)}) copy-start(s32[1,2,64]{2,1,0:T(2,128)} %param.13) | copy-start | bytes 1540
  185.0 2.7 copy-start.9
  205.5 6.4 %copy-start.11 = (bf16[128,512]{1,0:T(8,128)(2,1)S(1)}, bf16[128,512]{1,0:T(8,128)(2,1)}, u32[]{:S(2)}) copy-start(bf16[128,512]{1,0:T(8,128)(2,1)} %get-tuple-element.40) | copy-start | bytes 393220
  227.0 57.2 %all-to-all-start.3 = ((bf16[64,3,4096]{2,1,0:T(4,128)(2,1)}), bf16[64,3,4096]{2,1,0:T(4,128)(2,1)}, u32[]{:S(2)}, u32[]{:S(2)}) async-start(bf16[64,3,4096]{2,1,0:T(4,128)(2,1)} %reshape.425), calls=%async_computation.3 | async-start | bytes 4194304 | tf_op jit(solution)/shard_map/all_to_all | solution.py:122
  234.7 4.3 %copy-start.7 = (bf16[1,3,4,1024,128]{4,3,2,1,0:T(8,128)(2,1)S(1)}, bf16[1,3,4,1024,128]{4,3,2,1,0:T(8,128)(2,1)}, u32[]{:S(2)}) copy-start(bf16[1,3,4,1024,128]{4,3,2,1,0:T(8,128)(2,1)} %all-gather.2.cloned.1.call-done) | copy-start | bytes 9437188
  234.7 5.0 %copy-start.10 = (bf16[128,4,128,1]{2,1,0,3:T(4,128)(2,1)S(1)}, bf16[128,4,128,1]{2,1,0,3:T(4,128)(2,1)}, u32[]{:S(2)}) copy-start(bf16[128,4,128,1]{2,1,0,3:T(4,128)(2,1)} %copy-done.9) | copy-start | bytes 393220
  244.8 46.5 %copy-start.1 = (bf16[128,4096]{1,0:T(8,128)(2,1)S(1)}, bf16[128,4096]{1,0:T(8,128)(2,1)}, u32[]{:S(2)}) copy-start(bf16[128,4096]{1,0:T(8,128)(2,1)} %param.8) | copy-start | bytes 3145732
Sparse Core Ops, SparseCore 0:
  41.5 52.7 all-gather.1
  212.0 47.6 reduce-scatter.3
where the time goes:
time: 304 us; the launch traced here: 299 us
  waiting for transfers between devices  97.6 us (32%)
  blocking collectives  53.4 us (18%)
  local copies, waits for them, and re-layouts  46.9 us (15%)
  matrix products  45 us (15%)
  other arithmetic  23.7 us (8%)
  starting transfers between devices  17 us (6%)
  between operations  14.9 us (5%)
    all_to_all x1, waiting for transfers between devices, shards(): lax.all_to_all(send_grads, 'exp', split_axis=0, concat_axis=0, tiled=True)  45.6 us
    all_to_all x1, waiting for transfers between devices, shards(): lax.all_to_all(send_rows, 'exp', split_axis=0, concat_axis=0, tiled=True)  44.7 us
    psum x1, blocking collectives, shards(): mix_grad = lax.psum(mix_part, 'seq')  32.7 us
    all_to_all x1, blocking collectives, shards(): lax.all_to_all(wanted.reshape(peer_count, slot_cap), 'exp', split_axis=0,...  20.7 us
    unnamed x35, local copies, waits for them, and re-layouts  18 us
    another operation x2, other arithmetic  15 us
    dot_general x2, matrix products, contract(): lax.dot_general(left, right, (((0,), (0,)), ((), ())), preferred_element_...  7.55 us
    dot_general x3, matrix products, factored_grads(): jnp.einsum('rap,riaq->ipq', left_view.astype(jnp.float32), mixed_right, p...  7.17 us
  transfers between devices with their start and end apart: 5, of which 3 were waited for; matrix products, arithmetic and copies ran while one was open for 17% of the time, Pallas kernels for 0%

commit v1 on v0

v1 whole, which is shorter than its diff:
```python
import jax
import jax.numpy as jnp
from jax import lax
from jax.experimental import pallas as pl
from jax.experimental.pallas import tpu as pltpu
from jax.sharding import PartitionSpec as P

MESH = pl.DeviceIdType.MESH
BF = jnp.bfloat16
F32 = jnp.float32
I32 = jnp.int32
FWD = 8
RET = 4
AHEAD = 3


def dot(a, b):
    return lax.dot_general(a, b, (((1,), (0,)), ((), ())), preferred_element_type=F32)


def dot_nt(a, b):
    return lax.dot_general(a, b, (((1,), (1,)), ((), ())), preferred_element_type=F32)


def dot_tn(a, b):
    return lax.dot_general(a, b, (((0,), (0,)), ((), ())), preferred_element_type=F32)


def iota(shape, dim):
    return lax.broadcasted_iota(I32, shape, dim)


def each(n, body):
    lax.fori_loop(0, n, lambda d, carry: (body(d), carry)[1], 0)


def kernel(
    tok, cot, fac, mix, ints, tok_out, fac_out, mix_out, gate_out,
    selx, sely, pick, pick_t, chose, chose_t, perm,
    send1, recv1, send2, recv2, send3, recv3, send4, recv4,
    fbuf, xs, ybuf, ubuf, ends, gates, ggs, mdrow, mixbuf,
    plus_s, plus_r, minus_s, minus_r,
    selx_sem, sely_sem, y_sem, x_sem, bx_sem, by_sem, agp_sem, agm_sem, rsp_sem, rsm_sem, mix_sem,
):
    me = lax.axis_index("exp")
    z = lax.axis_index("seq")
    core, y, x = lax.rem(me, 2), lax.rem(me // 2, 8), me // 16
    g = x * 2 + core

    def at_y(d):
        return {"exp": (x * 8 + lax.rem(y + d + 1, 8)) * 2 + core, "seq": z}

    def at_g(d):
        o = lax.rem(g + d + 1, 8)
        return {"exp": ((o // 2) * 8 + y) * 2 + lax.rem(o, 2), "seq": z}

    def at_z(d):
        return {"exp": me, "seq": lax.rem(z + d + 1, 8)}

    def remote(src, dst, sems, where):
        return pltpu.make_async_remote_copy(
            src_ref=src, dst_ref=dst, send_sem=sems[0], recv_sem=sems[1],
            device_id=where, device_id_type=MESH,
        )

    barrier = pltpu.get_barrier_semaphore()
    for place in (at_g, at_y, at_z):
        each(7, lambda d, place=place: pl.semaphore_signal(barrier, inc=1, device_id=place(d), device_id_type=MESH))
    pl.semaphore_wait(barrier, 21)

    def selx_copy(d):
        return remote(selx.at[g], selx.at[g], (selx_sem.at[0, d], selx_sem.at[1, d]), at_g(d))

    selx[g] = ints[0]
    each(7, lambda d: selx_copy(d).start())

    for m in range(3):
        for i in range(4):
            fbuf[z, m, :, i * 128 : (i + 1) * 128] = fac[0, m, i]

    def agp_copy(s):
        slot = lax.rem(z - s + 8, 8)
        return remote(fbuf.at[slot], fbuf.at[slot], (agp_sem.at[0, s], agp_sem.at[1, s]), at_z(0))

    def agm_copy(s):
        slot = lax.rem(z + s, 8)
        return remote(fbuf.at[slot], fbuf.at[slot], (agm_sem.at[0, s], agm_sem.at[1, s]), at_z(6))

    agp_copy(0).start()
    agm_copy(0).start()

    eye = iota((128, 128), 0) == iota((128, 128), 1)
    lane = iota((1, 128), 1)

    def column(row):
        return jnp.sum(jnp.where(eye, jnp.broadcast_to(row, (128, 128)), 0.0), axis=1, keepdims=True)

    gate_row = jax.nn.sigmoid(ints[1][0:1].astype(F32) / 64.0)
    gates[...] = jnp.broadcast_to(column(gate_row), (128, 128))
    owner = lax.shift_right_logical(ints[0][0:1], 7) + jnp.where(lane >= 64, 32, 0)
    place = (lax.shift_right_logical(owner, 4) * 2 + (owner & 1)) * 48 + (lax.shift_right_logical(owner, 1) & 7)
    owner_row = owner.astype(F32)
    owner_col = column(owner_row)
    same = jnp.broadcast_to(owner_col, (128, 128)) == jnp.broadcast_to(owner_row, (128, 128))
    before = iota((128, 128), 0) < iota((128, 128), 1)
    after = iota((128, 128), 1) < iota((128, 128), 0)
    rank_row = jnp.sum(jnp.where(same & before, 1.0, 0.0), axis=0, keepdims=True)
    rank_col = jnp.sum(jnp.where(same & after, 1.0, 0.0), axis=1, keepdims=True)
    base_row = place + rank_row.astype(I32) * 8
    base_col = column(place.astype(F32)).astype(I32) + rank_col.astype(I32) * 8
    for t in range(2):
        hit = iota((128, 384), 1) == jnp.broadcast_to(base_col + 24 * t, (128, 384))
        chose[t * 128 : (t + 1) * 128, :] = jnp.where(hit, 1.0, 0.0).astype(BF)
        hit = iota((384, 128), 0) == jnp.broadcast_to(base_row + 24 * t, (384, 128))
        chose_t[:, t * 128 : (t + 1) * 128] = jnp.where(hit, 1.0, 0.0).astype(BF)
    for o in range(8):
        s = iota((48, 384), 0)
        hit = iota((48, 384), 1) == (s & 7) * 48 + (s - (s & 7)) + o
        perm[o * 48 : (o + 1) * 48, :] = jnp.where(hit, 1.0, 0.0).astype(BF)

    each(7, lambda d: selx_copy(d).wait())
    tile = jnp.zeros((8, 128), I32)
    for o in range(8):
        tile = jnp.where(iota((8, 128), 0) == o, selx[o], tile)
    sely[y] = tile

    def sely_copy(d):
        return remote(sely.at[y], sely.at[y], (sely_sem.at[0, d], sely_sem.at[1, d]), at_y(d))

    each(7, lambda d: sely_copy(d).start())
    each(7, lambda d: sely_copy(d).wait())

    block, own = me // 32, lax.rem(me, 32)
    local = sely[...].reshape(64, 128) - own * 128
    wide = iota((64, 128), 1)
    valid = (local >= 0) & (local < 128) & (lax.shift_right_logical(wide, 6) == block)
    lane_f = wide.astype(F32)
    first = jnp.min(jnp.where(valid, lane_f, 999.0), axis=1, keepdims=True)
    rank = lane_f - first
    wanted = [
        jnp.sum(jnp.where(valid & (rank == float(r)), local.astype(F32) + 1000.0, 0.0), axis=1, keepdims=True) - 1000.0
        for r in range(3)
    ]
    rows = []
    for o in range(8):
        for t in range(2):
            for r in range(3):
                want = jnp.broadcast_to(wanted[r][o * 8 : (o + 1) * 8] + 128.0 * t, (8, 256))
                rows.append(jnp.where(iota((8, 256), 1).astype(F32) == want, 1.0, 0.0))
    picked = jnp.concatenate(rows, axis=0)
    pick[...] = picked.astype(BF)
    pick_t[...] = picked.T.astype(BF)

    def y_copy(k, d):
        o = lax.rem(y + d + 1, 8)
        return remote(send1.at[k, o], recv1.at[k, y], (y_sem.at[0, k, d], y_sem.at[1, k, d]), at_y(d))

    def x_copy(k, d):
        o = lax.rem(g + d + 1, 8)
        return remote(send2.at[k, o], recv2.at[k, g], (x_sem.at[0, k, d], x_sem.at[1, k, d]), at_g(d))

    def send_y(k):
        cols = pl.ds(pl.multiple_of(k * 512, 512), 512)
        both = jnp.concatenate([tok[:, cols], cot[:, cols]], axis=0)
        send1[k] = dot(pick[...], both).astype(BF).reshape(8, 48, 512)
        each(7, lambda d: y_copy(k, d).start())
        recv1[k, y] = send1[k, y]

    def multiply(a):
        wide_rows = [
            jnp.concatenate([xs[t, 2 * a], xs[t, 2 * a + 1]], axis=1) for t in range(2)
        ]
        for m in range(3):
            ybuf[m, a] = dot(wide_rows[m // 2], fbuf[:, m].reshape(1024, 512))

    each(AHEAD, send_y)

    def forward(k):
        @pl.when(k < FWD)
        def _():
            each(7, lambda d: y_copy(k, d).wait_recv())
            send2[k] = dot(perm[...], recv1[k].reshape(384, 512)).astype(BF).reshape(8, 48, 512)
            each(7, lambda d: x_copy(k, d).start())
            recv2[k, g] = send2[k, g]

        @pl.when(k + AHEAD < FWD)
        def _():
            send_y(k + AHEAD)

        @pl.when(k < 4)
        def _():
            agp_copy(k).wait_recv()

            @pl.when(k < 3)
            def _():
                agp_copy(k + 1).start()
                agm_copy(k).wait_recv()

            @pl.when(k < 2)
            def _():
                agm_copy(k + 1).start()

        @pl.when(k > 0)
        def _():
            each(7, lambda d: x_copy(k - 1, d).wait_recv())
            both = dot(chose[...], recv2[k - 1].reshape(384, 512)).astype(BF)
            xs[0, k - 1] = both[:128]
            xs[1, k - 1] = both[128:]

        @pl.when(k == 4)
        def _():
            multiply(0)

        @pl.when((k >= 4) & (lax.rem(k, 2) == 0))
        def _():
            multiply(k // 2 - 1)

    each(FWD + 1, forward)

    def middle(block_of_rows):
        at = pl.ds(pl.multiple_of(block_of_rows * 32, 32), 32)

        def combine(m):
            outs = [None] * 4
            for a in range(4):
                for i in range(4):
                    v = ybuf[m, a, at, i * 128 : (i + 1) * 128]
                    for b in range(4):
                        term = mix[0, m, i, a, b] * v
                        outs[b] = term if outs[b] is None else outs[b] + term
            return outs

        gate = gates[at, :]
        pre_gate, pre_up, pulled = combine(0), combine(1), combine(2)
        inner = jnp.zeros((32, 128), F32)
        for b in range(4):
            s = jax.nn.sigmoid(pre_gate[b])
            act = pre_gate[b] * s
            slope = s + act * (1.0 - s)
            hidden = act * pre_up[b]
            inner = inner + hidden * pulled[b]
            back = gate * pulled[b]
            ends[0, b, at, :] = back * pre_up[b] * slope
            ends[1, b, at, :] = back * act
            ends[2, b, at, :] = gate * hidden
        ggs[at, :] = inner
        for m in range(3):
            parts = [ends[m, b, at, :] for b in range(4)]
            for a in range(4):
                for i in range(4):
                    total = mix[0, m, i, a, 0] * parts[0]
                    for b in range(1, 4):
                        total = total + mix[0, m, i, a, b] * parts[b]
                    ubuf[m, a, at, i * 128 : (i + 1) * 128] = total.astype(BF)

    each(4, middle)

    def bx_copy(k, d):
        o = lax.rem(g + d + 1, 8)
        return remote(send3.at[k, o], recv3.at[k, g], (bx_sem.at[0, k, d], bx_sem.at[1, k, d]), at_g(d))

    def by_copy(k, d):
        o = lax.rem(y + d + 1, 8)
        return remote(send4.at[k, o], recv4.at[k, y], (by_sem.at[0, k, d], by_sem.at[1, k, d]), at_y(d))

    def send_bx(a):
        both = jnp.concatenate(
            [
                dot_nt(ubuf[0, a], fbuf[4 * h : 4 * h + 4, 0].reshape(512, 512))
                + dot_nt(ubuf[1, a], fbuf[4 * h : 4 * h + 4, 1].reshape(512, 512))
                for h in range(2)
            ],
            axis=0,
        ).astype(BF)
        send3[a] = dot(chose_t[...], both).astype(BF).reshape(8, 48, 512)
        each(7, lambda d: bx_copy(a, d).start())
        recv3[a, g] = send3[a, g]

    def part(shard, m):
        half = shard // 4
        at = pl.ds(pl.multiple_of(lax.rem(shard, 4) * 128, 128), 128)
        left = jnp.concatenate([xs[m // 2, 2 * a + half, :, at] for a in range(4)], axis=0)
        return dot_tn(left, ubuf[m].reshape(512, 512))

    def rsp_copy(s):
        return remote(plus_s.at[s], plus_r.at[s], (rsp_sem.at[0, s], rsp_sem.at[1, s]), at_z(0))

    def rsm_copy(s):
        return remote(minus_s.at[s], minus_r.at[s], (rsm_sem.at[0, s], rsm_sem.at[1, s]), at_z(6))

    send_bx(0)
    for m in range(3):
        plus_s[0, m] = part(lax.rem(z + 4, 8), m).astype(BF)
    rsp_copy(0).start()
    for m in range(3):
        minus_s[0, m] = part(lax.rem(z + 5, 8), m).astype(BF)
    rsm_copy(0).start()
    each(RET - 1, lambda k: send_bx(k + 1))

    def back(k):
        each(7, lambda d: bx_copy(k, d).wait_recv())
        send4[k] = dot(perm[...], recv3[k].reshape(384, 512)).astype(BF).reshape(8, 48, 512)
        each(7, lambda d: by_copy(k, d).start())
        recv4[k, y] = send4[k, y]

    each(2, back)

    def dots(n):
        m, a = n // 4, lax.rem(n, 4)
        sums = []
        for i in range(4):
            v = ybuf[m, a, :, i * 128 : (i + 1) * 128]
            for b in range(4):
                sums.append(jnp.sum(v * ends[m, b], axis=0, keepdims=True))
        mdrow[pl.ds(pl.multiple_of(n * 16, 16), 16), :] = jnp.concatenate(sums, axis=0)

    mdrow[192:256, :] = jnp.zeros((64, 128), F32)
    each(12, dots)
    mixbuf[z] = lax.dot_general(
        jnp.ones((8, 128), F32), mdrow[...], (((1,), (1,)), ((), ())),
        preferred_element_type=F32, precision=lax.Precision.HIGHEST,
    )

    def mix_copy(d):
        return remote(mixbuf.at[z], mixbuf.at[z], (mix_sem.at[0, d], mix_sem.at[1, d]), at_z(d))

    each(7, lambda d: mix_copy(d).start())

    gate_col = gates[...]
    total_col = jnp.sum(ggs[...], axis=1, keepdims=True) * gate_col * (1.0 - gate_col)
    gate_out[...] = jnp.broadcast_to(jnp.sum(jnp.where(eye, total_col, 0.0), axis=0, keepdims=True), (8, 128))

    def reduce_step(s):
        rsp_copy(s).wait_recv()
        for m in range(3):
            plus_s[s + 1, m] = (part(lax.rem(z + 3 - s, 8), m) + plus_r[s, m].astype(F32)).astype(BF)
        rsp_copy(s + 1).start()

        @pl.when(s < 2)
        def _():
            rsm_copy(s).wait_recv()
            for m in range(3):
                minus_s[s + 1, m] = (part(lax.rem(z + 6 + s, 8), m) + minus_r[s, m].astype(F32)).astype(BF)
            rsm_copy(s + 1).start()

    def arrive(k):
        each(7, lambda d: by_copy(k, d).wait_recv())
        both = dot(pick_t[...], recv4[k].reshape(384, 512)).astype(BF)
        for h in range(2):
            tok_out[:, pl.ds(pl.multiple_of(k * 1024 + h * 512, 512), 512)] = both[h * 128 : (h + 1) * 128]

    reduce_step(0)
    back(2)
    back(3)
    each(2, lambda s: (arrive(s), reduce_step(s + 1)))
    each(2, lambda s: arrive(s + 2))
    rsp_copy(3).wait_recv()
    rsm_copy(2).wait_recv()
    for m in range(3):
        total = part(z, m) + plus_r[3, m].astype(F32) + minus_r[2, m].astype(F32)
        for i in range(4):
            fac_out[0, m, i] = total[:, i * 128 : (i + 1) * 128]

    each(7, lambda d: mix_copy(d).wait_recv())
    total = mixbuf[0]
    for o in range(1, 8):
        total = total + mixbuf[o]
    mix_out[...] = total

    each(7, lambda d: mix_copy(d).wait_send())
    each(FWD, lambda k: each(7, lambda d: (y_copy(k, d).wait_send(), x_copy(k, d).wait_send())))
    each(RET, lambda k: each(7, lambda d: (bx_copy(k, d).wait_send(), by_copy(k, d).wait_send())))
    each(4, lambda s: (agp_copy(s).wait_send(), rsp_copy(s).wait_send()))
    each(3, lambda s: (agm_copy(s).wait_send(), rsm_copy(s).wait_send()))


def shards(tokens, cotangent, factors, mix, selection, scores):
    ints = jnp.broadcast_to(
        jnp.concatenate([selection.reshape(1, 1, 128), scores.reshape(1, 1, 128)], axis=0), (2, 8, 128)
    )
    vmem = pl.BlockSpec(memory_space=pltpu.VMEM)
    dma = pltpu.SemaphoreType.DMA
    row = (8, 48, 512)
    token_grad, factor_grad, mixed, gated = pl.pallas_call(
        kernel,
        out_shape=(
            jax.ShapeDtypeStruct((128, 4096), BF),
            jax.ShapeDtypeStruct((1, 3, 4, 128, 128), F32),
            jax.ShapeDtypeStruct((8, 256), F32),
            jax.ShapeDtypeStruct((8, 128), F32),
        ),
        in_specs=[vmem, vmem, vmem, pl.BlockSpec(memory_space=pltpu.SMEM), vmem],
        out_specs=(vmem, vmem, vmem, vmem),
        scratch_shapes=[
            pltpu.VMEM((8, 8, 128), I32),
            pltpu.VMEM((8, 8, 128), I32),
            pltpu.VMEM((384, 256), BF),
            pltpu.VMEM((256, 384), BF),
            pltpu.VMEM((256, 384), BF),
            pltpu.VMEM((384, 256), BF),
            pltpu.VMEM((384, 384), BF),
            *[pltpu.VMEM((FWD,) + row, BF)] * 4,
            *[pltpu.VMEM((RET,) + row, BF)] * 4,
            pltpu.VMEM((8, 3, 128, 512), BF),
            pltpu.VMEM((2, FWD, 128, 512), BF),
            pltpu.VMEM((3, 4, 128, 512), F32),
            pltpu.VMEM((3, 4, 128, 512), BF),
            pltpu.VMEM((3, 4, 128, 128), F32),
            pltpu.VMEM((128, 128), F32),
            pltpu.VMEM((128, 128), F32),
            pltpu.VMEM((256, 128), F32),
            pltpu.VMEM((8, 8, 256), F32),
            *[pltpu.VMEM((4, 3, 128, 512), BF)] * 2,
            *[pltpu.VMEM((3, 3, 128, 512), BF)] * 2,
            dma((2, 7)),
            dma((2, 7)),
            dma((2, FWD, 7)),
            dma((2, FWD, 7)),
            dma((2, RET, 7)),
            dma((2, RET, 7)),
            dma((2, 4)),
            dma((2, 3)),
            dma((2, 4)),
            dma((2, 3)),
            dma((2, 7)),
        ],
        compiler_params=pltpu.CompilerParams(
            collective_id=0, has_side_effects=True, vmem_limit_bytes=58 << 20
        ),
    )(tokens, cotangent, factors, mix, ints)
    mix_grad = mixed[0, :192].reshape(1, 3, 4, 4, 4).transpose(0, 1, 3, 2, 4)
    return token_grad, factor_grad, mix_grad, gated[0].reshape(1, 2, 64)


def solution(mesh):
    return jax.shard_map(
        shards,
        mesh=mesh,
        in_specs=(
            P(("seq", "exp"), None),
            P(("seq", "exp"), None),
            P("exp", None, None, "seq", None),
            P("exp", None, None, None, None),
            P("exp", "seq", None),
            P("exp", "seq", None),
        ),
        out_specs=(
            P(("seq", "exp"), None),
            P("exp", None, None, "seq", None),
            P("exp", None, None, None, None),
            P("exp", "seq", None),
        ),
        check_vma=False,
    )
```

time: 304 us -> 166 us (0.55); the launches traced: 299 us -> 166 us
  Pallas kernels: 0 us -> 158 us
  waiting for transfers between devices: 97.6 us -> 0 us
  blocking collectives: 53.4 us -> 0 us
  matrix products: 45 us -> 0 us
  local copies, waits for them, and re-layouts: 46.9 us -> 7.49 us
  other arithmetic: 23.7 us -> 0.01 us
  starting transfers between devices: 17 us -> 0 us
  between operations: 14.9 us -> 0.65 us
    pallas_call x0 -> x1, Pallas kernels: none -> 158 us  [shards(): pl.pallas_call(kernel, out_shape=(jax.ShapeDtypeStruct((128, 4096), BF),...]
    all_to_all x3 -> x0, waiting for transfers between devices: 96.9 us -> none  [the longest x1 45.6 us: shards(): lax.all_to_all(send_grads, 'exp', split_axis=0, concat_axis=0, tiled=True)]
    dot_general x21 -> x0, matrix products: 45 us -> none  [the longest x2 7.55 us: contract(): lax.dot_general(left, right, (((0,), (0,)), ((), ())), preferred_element_...]
    psum x1 -> x0, blocking collectives: 32.7 us -> none  [shards(): mix_grad = lax.psum(mix_part, 'seq')]
    reshape x11 -> x2, local copies, waits for them, and re-layouts: 22.6 us -> 0.85 us  [the longest x1 0.77 us: shards(): selection.reshape(1, 1, 128)]
    all_to_all x1 -> x0, blocking collectives: 20.7 us -> none  [shards(): lax.all_to_all(wanted.reshape(peer_count, slot_cap), 'exp', split_axis=0,...]
    another operation x3 -> x0, other arithmetic: 17.1 us -> none
    all_to_all x3 -> x0, starting transfers between devices: 16.8 us -> none  [the longest x1 6.01 us: shards(): lax.all_to_all(send_grads, 'exp', split_axis=0, concat_axis=0, tiled=True)]
  transfers between devices with their start and end apart: 5 -> 0, of which waited for: 3 -> 0; matrix products, arithmetic and copies ran while one was open for 17% -> 0% of each run, Pallas kernels for 0% -> 0%
where the time goes in v1:
time: 166 us
  Pallas kernels  158 us (95%)
  local copies, waits for them, and re-layouts  7.49 us (5%)
    pallas_call x1, Pallas kernels, shards(): pl.pallas_call(kernel, out_shape=(jax.ShapeDtypeStruct((128, 4096), BF),...  158 us

profile of v1, /device:TPU:1, one launch (start us, length us, event | category | flops | bytes accessed | tf_op | source)
XLA Modules:
  0.0 166.0 jit_solution(5010490576697467053)
XLA Ops:
  0.6 0.0 copy-start.1
  0.6 0.8 reshape.14
  1.4 0.0 copy-done.1
  1.4 0.1 reshape.15
  1.5 0.6 broadcast_in_dim.8.ints
  2.1 157.8 %shard_map.93 = (bf16[128,4096]{1,0:T(8,128)(2,1)}, f32[1,3,4,128,128]{4,3,2,1,0:T(8,128)}, f32[8,256]{1,0:T(8,128)}, f32[8,128]{1,0:T(8,128)}) custom-call(bf16[128,4096]{1,0:T(8,128)(2,1)} %tok.1, bf16[128,4096]{1,0:T(8,128)(2,1)} %cot.1, bf16[1,3,4,128,128]{4,3,2,1,0:T(8,128)(2,1)} %fac.1, f32[1,3,4,4,4]{4,3,2,1,0:T(4,128)} %mix.1, ...), custom_call_target="tpu_custom_call" | custom-call | tf_op jit(solution)/shard_map/pallas_call | solution.py:384
  160.0 0.7 slice_reduce_fusion.1
  160.6 0.6 reshape_squeeze.7
  161.3 0.7 slice_reduce_fusion
  162.0 0.1 reshape_squeeze.6
  162.1 0.6 copy.12
  162.7 0.0 copy-start
  162.8 2.4 %copy.15 = bf16[128,4096]{1,0:T(8,128)(2,1)} copy(bf16[128,4096]{1,0:T(8,128)(2,1)} %get-tuple-element.16) | data formatting | bytes 2097152
  165.1 0.0 copy-done
  165.1 0.9 copy.16
  (1 shorter events, 0.0 us)
Async XLA Ops:
  0.6 0.8 copy-start.1
  162.7 2.4 %copy-start = (f32[1,3,4,128,128]{4,3,2,1,0:T(8,128)S(1)}, f32[1,3,4,128,128]{4,3,2,1,0:T(8,128)}, u32[]{:S(2)}) copy-start(f32[1,3,4,128,128]{4,3,2,1,0:T(8,128)} %get-tuple-element.17) | copy-start | bytes 2359300

commit v2 on v1

v2 whole, which is shorter than its diff:
```python
import jax
import jax.numpy as jnp
from jax import lax
from jax.experimental import pallas as pl
from jax.experimental.pallas import tpu as pltpu
from jax.sharding import PartitionSpec as P

MESH = pl.DeviceIdType.MESH
BF = jnp.bfloat16
F32 = jnp.float32
I32 = jnp.int32
FWD = 8
RET = 4
LATE = 6
AHEAD = 3


def dot(a, b):
    return lax.dot_general(a, b, (((1,), (0,)), ((), ())), preferred_element_type=F32)


def dot_nt(a, b):
    return lax.dot_general(a, b, (((1,), (1,)), ((), ())), preferred_element_type=F32)


def dot_tn(a, b):
    return lax.dot_general(a, b, (((0,), (0,)), ((), ())), preferred_element_type=F32)


def iota(shape, dim):
    return lax.broadcasted_iota(I32, shape, dim)


def each(n, body):
    lax.fori_loop(0, n, lambda d, carry: (body(d), carry)[1], 0)


def kernel(
    tok_in, cot_in, fac_in, mix_in, sel_in, sco_in, tok_out, fac_out, mix_out, gate_out,
    tok, cot, fac, mix, selection, scores, selx, sely, pick, pick_t, chose, chose_t, perm, pick2, pick2_t, chose2, chose2_t,
    send1, recv1, send2, recv2, send3, recv3, send4, recv4,
    fbuf, xs, ybuf, ubuf, ends, gates, ggs, mdrow, mixbuf,
    plus_s, plus_r, minus_s, minus_r,
    in_sem, selx_sem, sely_sem, y_sem, x_sem, bx_sem, by_sem, agp_sem, agm_sem, rsp_sem, rsm_sem, mix_sem,
):
    loads = [
        pltpu.make_async_copy(src, dst, in_sem.at[n])
        for n, (src, dst) in enumerate(
            ((sel_in, selection), (fac_in, fac), (tok_in, tok), (cot_in, cot), (sco_in, scores), (mix_in, mix))
        )
    ]
    for load in loads:
        load.start()
    me = lax.axis_index("exp")
    z = lax.axis_index("seq")
    core, y, x = lax.rem(me, 2), lax.rem(me // 2, 8), me // 16
    g = x * 2 + core

    def at_y(d):
        return {"exp": (x * 8 + lax.rem(y + d + 1, 8)) * 2 + core, "seq": z}

    def at_g(d):
        o = lax.rem(g + d + 1, 8)
        return {"exp": ((o // 2) * 8 + y) * 2 + lax.rem(o, 2), "seq": z}

    def at_z(d):
        return {"exp": me, "seq": lax.rem(z + d + 1, 8)}

    def remote(src, dst, sems, where):
        return pltpu.make_async_remote_copy(
            src_ref=src, dst_ref=dst, send_sem=sems[0], recv_sem=sems[1],
            device_id=where, device_id_type=MESH,
        )

    barrier = pltpu.get_barrier_semaphore()
    for place in (at_g, at_y, at_z):
        each(7, lambda d, place=place: pl.semaphore_signal(barrier, inc=1, device_id=place(d), device_id_type=MESH))
    for o in range(8):
        s = iota((48, 384), 0)
        hit = iota((48, 384), 1) == (s & 7) * 48 + (s - (s & 7)) + o
        perm[o * 48 : (o + 1) * 48, :] = jnp.where(hit, 1.0, 0.0).astype(BF)
    pl.semaphore_wait(barrier, 21)

    def selx_copy(d):
        return remote(selx.at[g], selx.at[g], (selx_sem.at[0, d], selx_sem.at[1, d]), at_g(d))

    def joined(ref):
        return jnp.concatenate([ref[0, 0:1], ref[0, 1:2]], axis=1)

    loads[0].wait()
    chosen = joined(selection)
    selx[g] = jnp.broadcast_to(chosen, (8, 128))
    each(7, lambda d: selx_copy(d).start())

    loads[1].wait()
    for m in range(3):
        for i in range(4):
            fbuf[z, m, :, i * 128 : (i + 1) * 128] = fac[0, m, i]

    def agp_copy(s):
        slot = lax.rem(z - s + 8, 8)
        return remote(fbuf.at[slot], fbuf.at[slot], (agp_sem.at[0, s], agp_sem.at[1, s]), at_z(0))

    def agm_copy(s):
        slot = lax.rem(z + s, 8)
        return remote(fbuf.at[slot], fbuf.at[slot], (agm_sem.at[0, s], agm_sem.at[1, s]), at_z(6))

    agp_copy(0).start()
    agm_copy(0).start()

    each(7, lambda d: selx_copy(d).wait())
    tile = jnp.zeros((8, 128), I32)
    for o in range(8):
        tile = jnp.where(iota((8, 128), 0) == o, selx[o], tile)
    sely[y] = tile

    def sely_copy(d):
        return remote(sely.at[y], sely.at[y], (sely_sem.at[0, d], sely_sem.at[1, d]), at_y(d))

    each(7, lambda d: sely_copy(d).start())
    eye = iota((128, 128), 0) == iota((128, 128), 1)
    lane = iota((1, 128), 1)

    def column(row):
        return jnp.sum(jnp.where(eye, jnp.broadcast_to(row, (128, 128)), 0.0), axis=1, keepdims=True)

    loads[4].wait()
    gate_row = jax.nn.sigmoid(joined(scores).astype(F32) / 64.0)
    gates[...] = jnp.broadcast_to(column(gate_row), (128, 128))
    owner = lax.shift_right_logical(chosen, 7) + jnp.where(lane >= 64, 32, 0)
    place = (lax.shift_right_logical(owner, 4) * 2 + (owner & 1)) * 48 + (lax.shift_right_logical(owner, 1) & 7)
    owner_row = owner.astype(F32)
    owner_col = column(owner_row)
    same = jnp.broadcast_to(owner_col, (128, 128)) == jnp.broadcast_to(owner_row, (128, 128))
    before = iota((128, 128), 0) < iota((128, 128), 1)
    after = iota((128, 128), 1) < iota((128, 128), 0)
    rank_row = jnp.sum(jnp.where(same & before, 1.0, 0.0), axis=0, keepdims=True)
    rank_col = jnp.sum(jnp.where(same & after, 1.0, 0.0), axis=1, keepdims=True)
    base_row = place + rank_row.astype(I32) * 8
    base_col = column(place.astype(F32)).astype(I32) + rank_col.astype(I32) * 8
    each(7, lambda d: sely_copy(d).wait())

    block, own = me // 32, lax.rem(me, 32)
    local = sely[...].reshape(64, 128) - own * 128
    wide = iota((64, 128), 1)
    valid = (local >= 0) & (local < 128) & (lax.shift_right_logical(wide, 6) == block)
    lane_f = wide.astype(F32)
    first = jnp.min(jnp.where(valid, lane_f, 999.0), axis=1, keepdims=True)
    rank = lane_f - first
    wanted = [
        jnp.sum(jnp.where(valid & (rank == float(r)), local.astype(F32) + 1000.0, 0.0), axis=1, keepdims=True) - 1000.0
        for r in range(3)
    ]
    rows = []
    for o in range(8):
        for t in range(2):
            for r in range(3):
                want = jnp.broadcast_to(wanted[r][o * 8 : (o + 1) * 8] + 128.0 * t, (8, 256))
                rows.append(jnp.where(iota((8, 256), 1).astype(F32) == want, 1.0, 0.0))
    picked = jnp.concatenate(rows, axis=0)
    pick[...] = picked.astype(BF)

    def y_copy(k, d, late):
        o = lax.rem(y + d + 1, 8)
        src, dst = (send2, recv2) if late else (send1, recv1)
        return remote(src.at[k, o], dst.at[k, y], (y_sem.at[0, k, d], y_sem.at[1, k, d]), at_y(d))

    def x_copy(k, d, late):
        o = lax.rem(g + d + 1, 8)
        src, dst = (send1, recv1) if late else (send2, recv2)
        return remote(src.at[k, o], dst.at[k, g], (x_sem.at[0, k, d], x_sem.at[1, k, d]), at_g(d))

    def first(k, late):
        cols = pl.ds(pl.multiple_of(k * 512, 512), 512)
        both = jnp.concatenate([tok[:, cols], cot[:, cols]], axis=0)
        send1[k] = dot((pick2 if late else pick)[...], both).astype(BF).reshape(8, 48, 512)
        copy, own = (x_copy, g) if late else (y_copy, y)
        each(7, lambda d: copy(k, d, late).start())
        recv1[k, own] = send1[k, own]

    def second(k, late):
        copy, then, own = (x_copy, y_copy, y) if late else (y_copy, x_copy, g)
        each(7, lambda d: copy(k, d, late).wait_recv())
        send2[k] = dot(perm[...], recv1[k].reshape(384, 512)).astype(BF).reshape(8, 48, 512)
        each(7, lambda d: then(k, d, late).start())
        recv2[k, own] = send2[k, own]

    def land(k, late):
        copy = y_copy if late else x_copy
        each(7, lambda d: copy(k, d, late).wait_recv())
        both = dot((chose2 if late else chose)[...], recv2[k].reshape(384, 512)).astype(BF)
        xs[0, k] = both[:128]
        xs[1, k] = both[128:]

    def multiply(k):
        a, h = k // 2, lax.rem(k, 2)
        for m in range(3):
            out = dot(xs[m // 2, k], fbuf[pl.ds(h * 4, 4), m].reshape(512, 512))

            @pl.when(h == 0)
            def _():
                ybuf[m, a] = out

            @pl.when(h == 1)
            def _():
                ybuf[m, a] += out

    loads[2].wait()
    loads[3].wait()
    first(0, False)
    first(1, False)
    pick2[...] = dot(perm[...], pick[...]).astype(BF)
    each(FWD - LATE, lambda k: first(k + LATE, True))
    first(2, False)
    for t in range(2):
        hit = iota((128, 384), 1) == jnp.broadcast_to(base_col + 24 * t, (128, 384))
        chose[t * 128 : (t + 1) * 128, :] = jnp.where(hit, 1.0, 0.0).astype(BF)
        hit = iota((384, 128), 0) == jnp.broadcast_to(base_row + 24 * t, (384, 128))
        chose_t[:, t * 128 : (t + 1) * 128] = jnp.where(hit, 1.0, 0.0).astype(BF)
    chose2[...] = dot(chose[...], perm[...]).astype(BF)
    chose2_t[...] = dot(perm[...], chose_t[...]).astype(BF)
    pick_t[...] = picked.T.astype(BF)
    pick2_t[...] = dot(pick_t[...], perm[...]).astype(BF)

    def forward(k):
        second(k, False)

        @pl.when(k + AHEAD < LATE)
        def _():
            first(k + AHEAD, False)

        @pl.when((k + AHEAD >= LATE) & (k + AHEAD < FWD))
        def _():
            second(k + AHEAD, True)

        @pl.when(k < 4)
        def _():
            agp_copy(k).wait_recv()

            @pl.when(k < 3)
            def _():
                agp_copy(k + 1).start()
                agm_copy(k).wait_recv()

            @pl.when(k < 2)
            def _():
                agm_copy(k + 1).start()

        @pl.when(k > 0)
        def _():
            land(k - 1, False)

        @pl.when(k == 4)
        def _():
            each(4, multiply)

        @pl.when(k == 5)
        def _():
            multiply(k - 1)

    each(LATE, forward)
    land(LATE - 1, False)
    multiply(LATE - 1)

    def finish(k):
        land(k + LATE, True)
        multiply(k + LATE)

    each(FWD - LATE, finish)

    loads[5].wait()

    def middle(block_of_rows):
        at = pl.ds(pl.multiple_of(block_of_rows * 32, 32), 32)

        def combine(m):
            outs = [None] * 4
            for a in range(4):
                for i in range(4):
                    v = ybuf[m, a, at, i * 128 : (i + 1) * 128]
                    for b in range(4):
                        term = mix[0, m, i, a, b] * v
                        outs[b] = term if outs[b] is None else outs[b] + term
            return outs

        gate = gates[at, :]
        pre_gate, pre_up, pulled = combine(0), combine(1), combine(2)
        inner = jnp.zeros((32, 128), F32)
        for b in range(4):
            s = jax.nn.sigmoid(pre_gate[b])
            act = pre_gate[b] * s
            slope = s + act * (1.0 - s)
            hidden = act * pre_up[b]
            inner = inner + hidden * pulled[b]
            back = gate * pulled[b]
            ends[0, b, at, :] = back * pre_up[b] * slope
            ends[1, b, at, :] = back * act
            ends[2, b, at, :] = gate * hidden
        ggs[at, :] = inner
        for m in range(3):
            parts = [ends[m, b, at, :] for b in range(4)]
            for a in range(4):
                for i in range(4):
                    total = mix[0, m, i, a, 0] * parts[0]
                    for b in range(1, 4):
                        total = total + mix[0, m, i, a, b] * parts[b]
                    ubuf[m, a, at, i * 128 : (i + 1) * 128] = total.astype(BF)

    each(4, middle)

    def bx_copy(k, d, early):
        o = lax.rem(g + d + 1, 8)
        src, dst = (send4, recv4) if early else (send3, recv3)
        return remote(src.at[k, o], dst.at[k, g], (bx_sem.at[0, k, d], bx_sem.at[1, k, d]), at_g(d))

    def by_copy(k, d, early):
        o = lax.rem(y + d + 1, 8)
        src, dst = (send3, recv3) if early else (send4, recv4)
        return remote(src.at[k, o], dst.at[k, y], (by_sem.at[0, k, d], by_sem.at[1, k, d]), at_y(d))

    def leave(a, early):
        both = jnp.concatenate(
            [
                dot_nt(ubuf[0, a], fbuf[4 * h : 4 * h + 4, 0].reshape(512, 512))
                + dot_nt(ubuf[1, a], fbuf[4 * h : 4 * h + 4, 1].reshape(512, 512))
                for h in range(2)
            ],
            axis=0,
        ).astype(BF)
        send3[a] = dot((chose2_t if early else chose_t)[...], both).astype(BF).reshape(8, 48, 512)
        copy, own = (by_copy, y) if early else (bx_copy, g)
        each(7, lambda d: copy(a, d, early).start())
        recv3[a, own] = send3[a, own]

    def turn(k, early):
        copy, then, own = (by_copy, bx_copy, g) if early else (bx_copy, by_copy, y)
        each(7, lambda d: copy(k, d, early).wait_recv())
        send4[k] = dot(perm[...], recv3[k].reshape(384, 512)).astype(BF).reshape(8, 48, 512)
        each(7, lambda d: then(k, d, early).start())
        recv4[k, own] = send4[k, own]

    def arrive(k, early):
        copy = bx_copy if early else by_copy
        each(7, lambda d: copy(k, d, early).wait_recv())
        both = dot((pick2_t if early else pick_t)[...], recv4[k].reshape(384, 512)).astype(BF)
        for h in range(2):
            tok_out[:, k * 1024 + h * 512 : k * 1024 + h * 512 + 512] = both[h * 128 : (h + 1) * 128]

    def part(shard, m):
        half = shard // 4
        at = pl.ds(pl.multiple_of(lax.rem(shard, 4) * 128, 128), 128)
        left = jnp.concatenate([xs[m // 2, 2 * a + half, :, at] for a in range(4)], axis=0)
        return dot_tn(left, ubuf[m].reshape(512, 512))

    def rs_copy(way, s, m):
        src, dst, sems = ((plus_s, plus_r, rsp_sem), (minus_s, minus_r, rsm_sem))[way]
        at = pl.ds(64 * way, 64) if s == 0 else pl.ds(0, 128)
        return remote(src.at[s, m, at], dst.at[s, m, at], (sems.at[0, s, m], sems.at[1, s, m]), at_z(6 * way))

    def reduce_first(m):
        far = part(lax.rem(z + 4, 8), m)
        for way, src in ((0, plus_s), (1, minus_s)):
            src[0, m, 64 * way : 64 * way + 64] = far[64 * way : 64 * way + 64].astype(BF)
            rs_copy(way, 0, m).start()

    def reduce_next(s, m):
        for way, src, got in ((0, plus_s, plus_r), (1, minus_s, minus_r)):
            own = part(lax.rem(z + 4 + (s if way else 8 - s), 8), m)
            rs_copy(way, s - 1, m).wait_recv()
            if s == 1:
                near = own[64 * way : 64 * way + 64] + got[0, m, 64 * way : 64 * way + 64].astype(F32)
                src[1, m, 64 * way : 64 * way + 64] = near.astype(BF)
                src[1, m, 64 - 64 * way : 128 - 64 * way] = own[64 - 64 * way : 128 - 64 * way].astype(BF)
            else:
                src[s, m] = (own + got[s - 1, m].astype(F32)).astype(BF)
            rs_copy(way, s, m).start()

    def reduce_last(m):
        total = part(z, m)
        rs_copy(0, 3, m).wait_recv()
        rs_copy(1, 3, m).wait_recv()
        total = total + plus_r[3, m].astype(F32) + minus_r[3, m].astype(F32)
        for i in range(4):
            fac_out[0, m, i] = total[:, i * 128 : (i + 1) * 128]

    def dots(n):
        m, a = n // 4, lax.rem(n, 4)
        for i in range(4):
            v = ybuf[m, a, :, i * 128 : (i + 1) * 128]
            for b in range(4):
                mdrow[b, pl.ds(m * 16 + i * 4 + a, 1), :] = jnp.sum(v * ends[m, b], axis=0, keepdims=True)

    def mix_copy(d):
        return remote(mixbuf.at[z], mixbuf.at[z], (mix_sem.at[0, d], mix_sem.at[1, d]), at_z(d))

    leave(0, True)
    leave(1, False)
    for m in range(3):
        reduce_first(m)
    leave(2, False)
    reduce_next(1, 0)
    turn(1, False)
    reduce_next(1, 1)
    reduce_next(1, 2)
    leave(3, False)
    reduce_next(2, 0)
    turn(0, True)
    turn(2, False)
    reduce_next(2, 1)
    reduce_next(2, 2)
    turn(3, False)
    arrive(0, True)
    reduce_next(3, 0)
    arrive(1, False)
    reduce_next(3, 1)
    reduce_next(3, 2)

    each(12, dots)
    small = jnp.zeros((48, 128), F32)
    for b in range(4):
        small = jnp.where(iota((48, 128), 1) == b, jnp.sum(mdrow[b], axis=1, keepdims=True), small)
    mixbuf[z] = small
    each(7, lambda d: mix_copy(d).start())
    gate_col = gates[...]
    total_col = jnp.sum(ggs[...], axis=1, keepdims=True) * gate_col * (1.0 - gate_col)
    total_row = jnp.sum(jnp.where(eye, total_col, 0.0), axis=0, keepdims=True)
    gate_out[0, 0:1] = total_row[:, :64]
    gate_out[0, 1:2] = total_row[:, 64:]

    reduce_last(0)
    arrive(2, False)
    reduce_last(1)
    reduce_last(2)
    each(7, lambda d: mix_copy(d).wait_recv())
    total = mixbuf[0]
    for o in range(1, 8):
        total = total + mixbuf[o]
    for m in range(3):
        for i in range(4):
            at = (m * 4 + i) * 4
            mix_out[0, m, i] = total[at : at + 4, :4]
    arrive(3, False)

    each(7, lambda d: mix_copy(d).wait_send())
    each(LATE, lambda k: each(7, lambda d: (y_copy(k, d, False).wait_send(), x_copy(k, d, False).wait_send())))
    each(FWD - LATE, lambda k: each(7, lambda d: (y_copy(k + LATE, d, True).wait_send(), x_copy(k + LATE, d, True).wait_send())))
    each(7, lambda d: (bx_copy(0, d, True).wait_send(), by_copy(0, d, True).wait_send()))
    each(RET - 1, lambda k: each(7, lambda d: (bx_copy(k + 1, d, False).wait_send(), by_copy(k + 1, d, False).wait_send())))
    each(4, lambda s: agp_copy(s).wait_send())
    each(3, lambda s: agm_copy(s).wait_send())
    for s in range(4):
        each(3, lambda m, s=s: (rs_copy(0, s, m).wait_send(), rs_copy(1, s, m).wait_send()))


def shards(tokens, cotangent, factors, mix, selection, scores):
    vmem = pl.BlockSpec(memory_space=pltpu.VMEM)
    hbm = pl.BlockSpec(memory_space=pltpu.HBM)
    dma = pltpu.SemaphoreType.DMA
    row = (8, 48, 512)
    return pl.pallas_call(
        kernel,
        out_shape=(
            jax.ShapeDtypeStruct((128, 4096), BF),
            jax.ShapeDtypeStruct((1, 3, 4, 128, 128), F32),
            jax.ShapeDtypeStruct((1, 3, 4, 4, 4), F32),
            jax.ShapeDtypeStruct((1, 2, 64), F32),
        ),
        in_specs=[hbm] * 6,
        out_specs=(vmem, vmem, vmem, vmem),
        scratch_shapes=[
            *[pltpu.VMEM((128, 4096), BF)] * 2,
            pltpu.VMEM((1, 3, 4, 128, 128), BF),
            pltpu.SMEM((1, 3, 4, 4, 4), F32),
            *[pltpu.VMEM((1, 2, 64), I32)] * 2,
            pltpu.VMEM((8, 8, 128), I32),
            pltpu.VMEM((8, 8, 128), I32),
            pltpu.VMEM((384, 256), BF),
            pltpu.VMEM((256, 384), BF),
            pltpu.VMEM((256, 384), BF),
            pltpu.VMEM((384, 256), BF),
            pltpu.VMEM((384, 384), BF),
            pltpu.VMEM((384, 256), BF),
            pltpu.VMEM((256, 384), BF),
            pltpu.VMEM((256, 384), BF),
            pltpu.VMEM((384, 256), BF),
            *[pltpu.VMEM((FWD,) + row, BF)] * 4,
            *[pltpu.VMEM((RET,) + row, BF)] * 4,
            pltpu.VMEM((8, 3, 128, 512), BF),
            pltpu.VMEM((2, FWD, 128, 512), BF),
            pltpu.VMEM((3, 4, 128, 512), F32),
            pltpu.VMEM((3, 4, 128, 512), BF),
            pltpu.VMEM((3, 4, 128, 128), F32),
            pltpu.VMEM((128, 128), F32),
            pltpu.VMEM((128, 128), F32),
            pltpu.VMEM((4, 48, 128), F32),
            pltpu.VMEM((8, 48, 128), F32),
            *[pltpu.VMEM((4, 3, 128, 512), BF)] * 4,
            dma((6,)),
            dma((2, 7)),
            dma((2, 7)),
            dma((2, FWD, 7)),
            dma((2, FWD, 7)),
            dma((2, RET, 7)),
            dma((2, RET, 7)),
            dma((2, 4)),
            dma((2, 3)),
            dma((2, 4, 3)),
            dma((2, 4, 3)),
            dma((2, 7)),
        ],
        compiler_params=pltpu.CompilerParams(
            collective_id=0, has_side_effects=True, vmem_limit_bytes=46 << 20
        ),
    )(*[pltpu.with_memory_space_constraint(v, pltpu.HBM) for v in (tokens, cotangent, factors, mix, selection, scores)])


def solution(mesh):
    return jax.shard_map(
        shards,
        mesh=mesh,
        in_specs=(
            P(("seq", "exp"), None),
            P(("seq", "exp"), None),
            P("exp", None, None, "seq", None),
            P("exp", None, None, None, None),
            P("exp", "seq", None),
            P("exp", "seq", None),
        ),
        out_specs=(
            P(("seq", "exp"), None),
            P("exp", None, None, "seq", None),
            P("exp", None, None, None, None),
            P("exp", "seq", None),
        ),
        check_vma=False,
    )
```

time: 166 us -> 145 us (0.87)
  Pallas kernels: 158 us -> 141 us
  local copies, waits for them, and re-layouts: 7.49 us -> 3.02 us
    pallas_call x1, Pallas kernels: 158 us -> 141 us  [shards(): pl.pallas_call(kernel, out_shape=(jax.ShapeDtypeStruct((128, 4096), BF),...]
where the time goes in v2:
time: 145 us; the launch traced here: 144 us
  Pallas kernels  141 us (97%)
  local copies, waits for them, and re-layouts  3.02 us (2%)
    pallas_call x1, Pallas kernels, shards(): pl.pallas_call(kernel, out_shape=(jax.ShapeDtypeStruct((128, 4096), BF),...  141 us
    unnamed x4, local copies, waits for them, and re-layouts  3.02 us

profile of v2, /device:TPU:1, one launch (start us, length us, event | category | flops | bytes accessed | tf_op | source)
XLA Modules:
  0.0 144.5 jit_solution(9635088382452344990)
XLA Ops:
  0.6 140.8 %shard_map.93 = (bf16[128,4096]{1,0:T(8,128)(2,1)S(1)}, f32[1,3,4,128,128]{4,3,2,1,0:T(8,128)S(1)}, f32[1,3,4,4,4]{4,3,2,1,0:T(4,128)S(1)}, f32[1,2,64]{2,1,0:T(2,128)S(1)}) custom-call(bf16[128,4096]{1,0:T(8,128)(2,1)} %tok_in.1, bf16[128,4096]{1,0:T(8,128)(2,1)} %cot_in.1, bf16[1,3,4,128,128]{4,3,2,1,0:T(8,128)(2,1)} %fac_in.1, f32[1,3,4,4,4]{4,3,2,1,0:T(4,128)} %mix_in.1, ...), custom_call_target="tpu_custom_call" | custom-call | tf_op jit(solution)/shard_map/pallas_call | solution.py:460
  141.4 1.0 copy.14
  142.4 0.9 copy.15
  143.3 0.6 copy.16
  143.9 0.6 copy.17

commit v3 on v2

--- a/solution.py
+++ b/solution.py
@@ -11,6 +11,7 @@
 I32 = jnp.int32
 FWD = 8
 RET = 4
+EARLY = 2
 LATE = 6
 AHEAD = 3
 
@@ -92,22 +93,6 @@
     selx[g] = jnp.broadcast_to(chosen, (8, 128))
     each(7, lambda d: selx_copy(d).start())
 
-    loads[1].wait()
-    for m in range(3):
-        for i in range(4):
-            fbuf[z, m, :, i * 128 : (i + 1) * 128] = fac[0, m, i]
-
-    def agp_copy(s):
-        slot = lax.rem(z - s + 8, 8)
-        return remote(fbuf.at[slot], fbuf.at[slot], (agp_sem.at[0, s], agp_sem.at[1, s]), at_z(0))
-
-    def agm_copy(s):
-        slot = lax.rem(z + s, 8)
-        return remote(fbuf.at[slot], fbuf.at[slot], (agm_sem.at[0, s], agm_sem.at[1, s]), at_z(6))
-
-    agp_copy(0).start()
-    agm_copy(0).start()
-
     each(7, lambda d: selx_copy(d).wait())
     tile = jnp.zeros((8, 128), I32)
     for o in range(8):
@@ -118,6 +103,23 @@
         return remote(sely.at[y], sely.at[y], (sely_sem.at[0, d], sely_sem.at[1, d]), at_y(d))
 
     each(7, lambda d: sely_copy(d).start())
+
+    loads[1].wait()
+    for m in range(3):
+        for i in range(4):
+            fbuf[z, m, :, i * 128 : (i + 1) * 128] = fac[0, m, i]
+
+    def agp_copy(s):
+        slot = lax.rem(z - s + 8, 8)
+        return remote(fbuf.at[slot], fbuf.at[slot], (agp_sem.at[0, s], agp_sem.at[1, s]), at_z(0))
+
+    def agm_copy(s):
+        slot = lax.rem(z + s, 8)
+        return remote(fbuf.at[slot], fbuf.at[slot], (agm_sem.at[0, s], agm_sem.at[1, s]), at_z(6))
+
+    agp_copy(0).start()
+    agm_copy(0).start()
+
     eye = iota((128, 128), 0) == iota((128, 128), 1)
     lane = iota((1, 128), 1)
 
@@ -394,24 +396,24 @@
         return remote(mixbuf.at[z], mixbuf.at[z], (mix_sem.at[0, d], mix_sem.at[1, d]), at_z(d))
 
     leave(0, True)
-    leave(1, False)
-    for m in range(3):
-        reduce_first(m)
+    reduce_first(0)
+    reduce_first(1)
+    reduce_first(2)
+    leave(1, True)
+    reduce_next(1, 0)
     leave(2, False)
-    reduce_next(1, 0)
-    turn(1, False)
     reduce_next(1, 1)
     reduce_next(1, 2)
     leave(3, False)
+    turn(2, False)
     reduce_next(2, 0)
     turn(0, True)
-    turn(2, False)
+    turn(3, False)
     reduce_next(2, 1)
     reduce_next(2, 2)
-    turn(3, False)
     arrive(0, True)
     reduce_next(3, 0)
-    arrive(1, False)
+    turn(1, True)
     reduce_next(3, 1)
     reduce_next(3, 2)
 
@@ -427,10 +429,10 @@
     gate_out[0, 0:1] = total_row[:, :64]
     gate_out[0, 1:2] = total_row[:, 64:]
 
+    arrive(1, True)
     reduce_last(0)
+    reduce_last(1)
     arrive(2, False)
-    reduce_last(1)
-    reduce_last(2)
     each(7, lambda d: mix_copy(d).wait_recv())
     total = mixbuf[0]
     for o in range(1, 8):
@@ -439,17 +441,26 @@
         for i in range(4):
             at = (m * 4 + i) * 4
             mix_out[0, m, i] = total[at : at + 4, :4]
+    reduce_last(2)
     arrive(3, False)
 
     each(7, lambda d: mix_copy(d).wait_send())
     each(LATE, lambda k: each(7, lambda d: (y_copy(k, d, False).wait_send(), x_copy(k, d, False).wait_send())))
     each(FWD - LATE, lambda k: each(7, lambda d: (y_copy(k + LATE, d, True).wait_send(), x_copy(k + LATE, d, True).wait_send())))
-    each(7, lambda d: (bx_copy(0, d, True).wait_send(), by_copy(0, d, True).wait_send()))
-    each(RET - 1, lambda k: each(7, lambda d: (bx_copy(k + 1, d, False).wait_send(), by_copy(k + 1, d, False).wait_send())))
+    each(EARLY, lambda k: each(7, lambda d: (bx_copy(k, d, True).wait_send(), by_copy(k, d, True).wait_send())))
+    each(RET - EARLY, lambda k: each(7, lambda d: (bx_copy(k + EARLY, d, False).wait_send(), by_copy(k + EARLY, d, False).wait_send())))
     each(4, lambda s: agp_copy(s).wait_send())
     each(3, lambda s: agm_copy(s).wait_send())
     for s in range(4):
         each(3, lambda m, s=s: (rs_copy(0, s, m).wait_send(), rs_copy(1, s, m).wait_send()))
+
+
+def write(*refs):
+    copies = [pltpu.make_async_copy(refs[n], refs[n + 4], refs[8].at[n]) for n in range(4)]
+    for copy in copies:
+        copy.start()
+    for copy in copies:
+        copy.wait()
 
 
 def shards(tokens, cotangent, factors, mix, selection, scores):
@@ -457,14 +468,15 @@
     hbm = pl.BlockSpec(memory_space=pltpu.HBM)
     dma = pltpu.SemaphoreType.DMA
     row = (8, 48, 512)
-    return pl.pallas_call(
+    outs = (
+        jax.ShapeDtypeStruct((128, 4096), BF),
+        jax.ShapeDtypeStruct((1, 3, 4, 128, 128), F32),
+        jax.ShapeDtypeStruct((1, 3, 4, 4, 4), F32),
+        jax.ShapeDtypeStruct((1, 2, 64), F32),
+    )
+    results = pl.pallas_call(
         kernel,
-        out_shape=(
-            jax.ShapeDtypeStruct((128, 4096), BF),
-            jax.ShapeDtypeStruct((1, 3, 4, 128, 128), F32),
-            jax.ShapeDtypeStruct((1, 3, 4, 4, 4), F32),
-            jax.ShapeDtypeStruct((1, 2, 64), F32),
-        ),
+        out_shape=outs,
         in_specs=[hbm] * 6,
         out_specs=(vmem, vmem, vmem, vmem),
         scratch_shapes=[
@@ -512,6 +524,13 @@
             collective_id=0, has_side_effects=True, vmem_limit_bytes=46 << 20
         ),
     )(*[pltpu.with_memory_space_constraint(v, pltpu.HBM) for v in (tokens, cotangent, factors, mix, selection, scores)])
+    return pl.pallas_call(
+        write,
+        out_shape=outs,
+        in_specs=[vmem] * 4,
+        out_specs=(pl.BlockSpec(memory_space=pl.ANY),) * 4,
+        scratch_shapes=[dma((4,))],
+    )(*[pltpu.with_memory_space_constraint(v, pltpu.VMEM) for v in results])
 
 
 def solution(mesh):

time: 145 us -> 143 us (0.986)
  local copies, waits for them, and re-layouts: 3.02 us -> 0 us
    unnamed x4 -> x0, local copies, waits for them, and re-layouts: 3.02 us -> none
    pallas_call x1 -> x2, Pallas kernels: 141 us -> 142 us  [the longest x1 141 us: shards(): pl.pallas_call(kernel, out_shape=outs, in_specs=[hbm] * 6, out_specs=(vme...]
where the time goes in v3:
time: 143 us
  Pallas kernels  142 us (99%)
    pallas_call x1, Pallas kernels, shards(): pl.pallas_call(kernel, out_shape=outs, in_specs=[hbm] * 6, out_specs=(vme...  141 us

profile of v3, /device:TPU:1, one launch (start us, length us, event | category | flops | bytes accessed | tf_op | source)
XLA Modules:
  0.0 142.8 jit_solution(9863485870972042991)
XLA Ops:
  0.6 140.9 %shard_map.93 = (bf16[128,4096]{1,0:T(8,128)(2,1)S(1)}, f32[1,3,4,128,128]{4,3,2,1,0:T(8,128)S(1)}, f32[1,3,4,4,4]{4,3,2,1,0:T(4,128)S(1)}, f32[1,2,64]{2,1,0:T(2,128)S(1)}) custom-call(bf16[128,4096]{1,0:T(8,128)(2,1)} %tok_in.1, bf16[128,4096]{1,0:T(8,128)(2,1)} %cot_in.1, bf16[1,3,4,128,128]{4,3,2,1,0:T(8,128)(2,1)} %fac_in.1, f32[1,3,4,4,4]{4,3,2,1,0:T(4,128)} %mix_in.1, ...), custom_call_target="tpu_custom_call" | custom-call | tf_op jit(solution)/shard_map/pallas_call | solution.py:477
  141.5 1.3 shard_map.94

commit v4 on v3

--- a/solution.py
+++ b/solution.py
@@ -299,16 +299,19 @@
             ends[1, b, at, :] = back * act
             ends[2, b, at, :] = gate * hidden
         ggs[at, :] = inner
-        for m in range(3):
-            parts = [ends[m, b, at, :] for b in range(4)]
-            for a in range(4):
-                for i in range(4):
-                    total = mix[0, m, i, a, 0] * parts[0]
-                    for b in range(1, 4):
-                        total = total + mix[0, m, i, a, b] * parts[b]
-                    ubuf[m, a, at, i * 128 : (i + 1) * 128] = total.astype(BF)
+
+    def spread(m, a):
+        for at in range(0, 128, 32):
+            parts = [ends[m, b, at : at + 32, :] for b in range(4)]
+            for i in range(4):
+                total = mix[0, m, i, a, 0] * parts[0]
+                for b in range(1, 4):
+                    total = total + mix[0, m, i, a, b] * parts[b]
+                ubuf[m, a, at : at + 32, i * 128 : (i + 1) * 128] = total.astype(BF)
 
     each(4, middle)
+    spread(0, 0)
+    spread(1, 0)
 
     def bx_copy(k, d, early):
         o = lax.rem(g + d + 1, 8)
@@ -396,6 +399,8 @@
         return remote(mixbuf.at[z], mixbuf.at[z], (mix_sem.at[0, d], mix_sem.at[1, d]), at_z(d))
 
     leave(0, True)
+    each(3, lambda n: (spread(0, n + 1), spread(1, n + 1)))
+    each(4, lambda n: spread(2, n))
     reduce_first(0)
     reduce_first(1)
     reduce_first(2)
@@ -405,14 +410,14 @@
     reduce_next(1, 1)
     reduce_next(1, 2)
     leave(3, False)
+    reduce_next(2, 0)
     turn(2, False)
-    reduce_next(2, 0)
+    reduce_next(2, 1)
     turn(0, True)
+    reduce_next(2, 2)
     turn(3, False)
-    reduce_next(2, 1)
-    reduce_next(2, 2)
+    reduce_next(3, 0)
     arrive(0, True)
-    reduce_next(3, 0)
     turn(1, True)
     reduce_next(3, 1)
     reduce_next(3, 2)
@@ -432,7 +437,7 @@
     arrive(1, True)
     reduce_last(0)
     reduce_last(1)
-    arrive(2, False)
+    reduce_last(2)
     each(7, lambda d: mix_copy(d).wait_recv())
     total = mixbuf[0]
     for o in range(1, 8):
@@ -441,7 +446,7 @@
         for i in range(4):
             at = (m * 4 + i) * 4
             mix_out[0, m, i] = total[at : at + 4, :4]
-    reduce_last(2)
+    arrive(2, False)
     arrive(3, False)
 
     each(7, lambda d: mix_copy(d).wait_send())

time: 143 us -> 140 us (0.979)
  Pallas kernels: 142 us -> 140 us
    pallas_call x1, Pallas kernels: 141 us -> 138 us  [shards(): pl.pallas_call(kernel, out_shape=outs, in_specs=[hbm] * 6, out_specs=(vme...]
where the time goes in v4:
time: 140 us
  Pallas kernels  140 us (100%)
    pallas_call x1, Pallas kernels, shards(): pl.pallas_call(kernel, out_shape=outs, in_specs=[hbm] * 6, out_specs=(vme...  138 us

profile of v4, /device:TPU:1, one launch (start us, length us, event | category | flops | bytes accessed | tf_op | source)
XLA Modules:
  0.0 140.3 jit_solution(10282493602229160531)
XLA Ops:
  0.6 138.4 %shard_map.93 = (bf16[128,4096]{1,0:T(8,128)(2,1)S(1)}, f32[1,3,4,128,128]{4,3,2,1,0:T(8,128)S(1)}, f32[1,3,4,4,4]{4,3,2,1,0:T(4,128)S(1)}, f32[1,2,64]{2,1,0:T(2,128)S(1)}) custom-call(bf16[128,4096]{1,0:T(8,128)(2,1)} %tok_in.1, bf16[128,4096]{1,0:T(8,128)(2,1)} %cot_in.1, bf16[1,3,4,128,128]{4,3,2,1,0:T(8,128)(2,1)} %fac_in.1, f32[1,3,4,4,4]{4,3,2,1,0:T(4,128)} %mix_in.1, ...), custom_call_target="tpu_custom_call" | custom-call | tf_op jit(solution)/shard_map/pallas_call | solution.py:482
  139.1 1.3 shard_map.94
